TPU v7x, 32 devices: a whole 2x2x4 slice. The times are simulated.
32 devices in a mesh: row: 4 (over y, x), col: 8 (over z, core).
Axes of the slice: x: 2, y: 2, z: 4, core: 2. Of those that a mesh axis runs over, the one named last changes fastest.
Arguments:
- node_features: bfloat16 [4096, 1024], P(('row', 'col')), may hold values from -6 to 6
- norm_gain: float32 [1024], replicated, may hold values from 0.5 to 1.5
- w_query: bfloat16 [1024, 1024], replicated, may hold values from -0.1875 to 0.1875
- w_keyvalue: bfloat16 [1024, 2048], replicated, may hold values from -0.1875 to 0.1875
- w_out: bfloat16 [1024, 1024], replicated, may hold values from -0.1875 to 0.1875
- bias_table: float32 [32, 8], replicated, may hold values from -4 to 4
- edge_slope: float32 [8], replicated, may hold values from 0.5 to 1.5
- pair_blocks: int32 [4, 8, 2, 16], P('row', 'col'), may hold values from -1 to 7, as said below
- bucket_ids: int32 [4, 8, 16, 128, 128], P('row', 'col'), may hold values from 0 to 31
- edge_weight: bfloat16 [4, 8, 4, 4, 128, 128], P('row', 'col'), may hold values from -4 to 240
Outputs:
- node_out: bfloat16 [4096, 1024], P(('row', 'col'))
Inputs may be any that keep to these rules, and one draw needn't show every extreme that they name: `pair_blocks`: slots of a tile with query block -1 are empty and name key block 0. The listed pairs of a tile are distinct; each tile (r, c) lists, among the slots from t = r, every block of node shard r * 8 + c paired with itself. Up to 4 slots from one owner to one row range are used, and some tile uses all 16 of its slots.
All inputs are finite; a program needn't handle non-finite values.
Results may differ from a plain program's by a relative error of at most 0.005.
Values may be sent and summed in bfloat16 or wider, within the bound.
A program may use at most 256 MiB of HBM per device.

v0:
```python
import math
import jax
import jax.numpy as jnp
from jax import lax
from jax.sharding import PartitionSpec as P

EPSILON = 1e-05
LOW_FLOOR = -1e30


def normalize(features, gain_vec):
    as_float = features.astype(jnp.float32)
    centered = as_float - jnp.mean(as_float, axis=-1, keepdims=True)
    variance = jnp.mean(centered * centered, axis=-1, keepdims=True)
    return (centered * lax.rsqrt(variance + EPSILON) * gain_vec).astype(jnp.bfloat16)


def local(
    node_features,
    norm_gain,
    w_query,
    w_keyvalue,
    w_out,
    bias_table,
    edge_slope,
    pair_blocks,
    bucket_ids,
    edge_weight,
):
    rows_own, model_width = node_features.shape
    head_count = edge_slope.shape[0]
    head_dim = model_width // head_count
    tile_size = bucket_ids.shape[-1]
    bucket_count = bias_table.shape[0]
    normalized = normalize(node_features, norm_gain)
    queries = jnp.dot(normalized, w_query, preferred_element_type=jnp.float32).astype(jnp.bfloat16)
    query_range = lax.all_gather(queries, "col", axis=0, tiled=True)
    key_value = jnp.dot(normalized, w_keyvalue, preferred_element_type=jnp.float32).astype(
        jnp.bfloat16
    )
    key_group = lax.all_gather(key_value, "row", axis=0, tiled=True)
    arrived = lax.all_to_all(edge_weight, "row", split_axis=2, concat_axis=0, tiled=True)
    slot_count = arrived.shape[0] * arrived.shape[3]
    edge_values = arrived.reshape(slot_count, tile_size, tile_size)
    pair_table = pair_blocks.reshape(2, slot_count)
    bucket_tiles = bucket_ids.reshape(slot_count, tile_size, tile_size)
    query_count = query_range.shape[0] // tile_size
    slot_cap = slot_count // lax.axis_size("row")
    key_blocks = rows_own // tile_size
    query_block = pair_table[0]
    key_block = pair_table[1] + jnp.arange(slot_count, dtype=jnp.int32) // slot_cap * key_blocks
    query_flat = query_range.reshape(query_count, tile_size * model_width)
    key_count = key_group.shape[0] // tile_size
    key_flat = key_group.reshape(key_count, tile_size * 2 * model_width)
    query_ids = jnp.arange(query_count, dtype=jnp.int32)
    key_ids = jnp.arange(key_count, dtype=jnp.int32)
    bucket_range = jnp.arange(bucket_count, dtype=jnp.int32)
    batch_size = math.gcd(slot_count, max(1, 512 // tile_size))
    turn_count = slot_count // batch_size
    score_scale = head_dim ** (-0.5)

    def score_slots(inputs):
        query_index, key_index, tile_weights, tile_buckets = inputs
        query_pick = (jnp.maximum(query_index, 0)[:, None] == query_ids[None, :]).astype(
            jnp.bfloat16
        )
        key_pick = (key_index[:, None] == key_ids[None, :]).astype(jnp.bfloat16)
        query_sel = jnp.dot(query_pick, query_flat, preferred_element_type=jnp.float32).astype(
            jnp.bfloat16
        )
        query_sel = query_sel.reshape(batch_size, tile_size, head_count, head_dim)
        pair_sel = jnp.dot(key_pick, key_flat, preferred_element_type=jnp.float32).astype(
            jnp.bfloat16
        )
        pair_sel = pair_sel.reshape(batch_size, tile_size, 2, head_count, head_dim)
        key_sel = pair_sel[:, :, 0]
        value_sel = pair_sel[:, :, 1]
        raw_score = (
            jnp.einsum("sihd,sjhd->shij", query_sel, key_sel, preferred_element_type=jnp.float32)
            * score_scale
        )
        bucket_hot = (tile_buckets[..., None] == bucket_range).astype(jnp.float32)
        lookup = jnp.einsum(
            "sijb,bh->shij", bucket_hot, bias_table, precision=lax.Precision.HIGHEST
        )
        raw_score = (
            raw_score
            + lookup
            + edge_slope[None, :, None, None] * tile_weights.astype(jnp.float32)[:, None]
        )
        row_max = jnp.max(raw_score, axis=-1)
        prob_vals = jnp.exp(raw_score - row_max[..., None]).astype(jnp.bfloat16)
        row_sum = jnp.sum(prob_vals.astype(jnp.float32), axis=-1)
        weighted = jnp.einsum(
            "shij,sjhd->sihd", prob_vals, value_sel, preferred_element_type=jnp.float32
        )
        return (row_max, row_sum, weighted)

    row_max, row_sum, weighted = lax.map(
        score_slots,
        (
            query_block.reshape(turn_count, batch_size),
            key_block.reshape(turn_count, batch_size),
            edge_values.reshape(turn_count, batch_size, tile_size, tile_size),
            bucket_tiles.reshape(turn_count, batch_size, tile_size, tile_size),
        ),
    )
    row_max = row_max.reshape(slot_count, head_count, tile_size)
    row_sum = row_sum.reshape(slot_count, head_count, tile_size)
    weighted = weighted.reshape(slot_count, tile_size, head_count, head_dim)
    member = query_block[None, :] == query_ids[:, None]
    chosen = member.astype(jnp.float32)
    block_max = jnp.max(jnp.where(member[:, :, None, None], row_max[None], LOW_FLOOR), axis=1)
    slot_max = jnp.einsum("qs,qhi->shi", chosen, block_max, precision=lax.Precision.HIGHEST)
    slot_live = (query_block >= 0)[:, None, None]
    factor = jnp.where(slot_live, jnp.exp(jnp.where(slot_live, row_max - slot_max, 0.0)), 0.0)
    block_sum = jnp.einsum("qs,shi->qih", chosen, factor * row_sum, precision=lax.Precision.HIGHEST)
    block_out = jnp.einsum(
        "qs,sihd->qihd",
        chosen,
        jnp.transpose(factor, (0, 2, 1))[..., None] * weighted,
        precision=lax.Precision.HIGHEST,
    )
    range_rows = query_count * tile_size
    max_rows = jnp.transpose(block_max, (0, 2, 1)).reshape(range_rows, head_count)
    sum_rows = block_sum.reshape(range_rows, head_count)
    out_rows = block_out.reshape(range_rows, head_count, head_dim)
    col_max, col_sum, col_out = (
        lax.all_to_all(max_rows[None], "col", split_axis=1, concat_axis=0, tiled=True),
        lax.all_to_all(sum_rows[None], "col", split_axis=1, concat_axis=0, tiled=True),
        lax.all_to_all(out_rows[None], "col", split_axis=1, concat_axis=0, tiled=True),
    )
    global_max = jnp.max(col_max, axis=0)
    col_factor = jnp.exp(col_max - global_max[None])
    mine_sum = jnp.sum(col_factor * col_sum, axis=0)
    mine_out = jnp.sum(col_factor[..., None] * col_out, axis=0)
    attention = (mine_out / mine_sum[..., None]).reshape(rows_own, model_width).astype(jnp.bfloat16)
    update = jnp.dot(attention, w_out, preferred_element_type=jnp.float32)
    return (node_features.astype(jnp.float32) + update).astype(jnp.bfloat16)


def solution(mesh):
    return jax.shard_map(
        local,
        mesh=mesh,
        in_specs=(
            P(("row", "col"), None),
            P(),
            P(),
            P(),
            P(),
            P(),
            P(),
            P("row", "col", None, None),
            P("row", "col", None, None, None),
            P("row", "col", None, None, None, None),
        ),
        out_specs=P(("row", "col"), None),
        check_vma=False,
    )
```

profile of v0, /device:TPU:0, one launch (start us, length us, event | category | flops | bytes accessed | tf_op | source)
XLA Modules:
  0.0 315.5 jit_solution(13089731285216129570)
XLA Ops:
  6.5 1.2 convert_reduce_fusion.1
  7.8 1.2 fusion.28
  9.0 3.9 %convolution_convert_fusion.2 = bf16[128,2048]{1,0:T(8,128)(2,1)} fusion(bf16[1024,2048]{1,0:T(8,128)(2,1)} %param.15, bf16[128,1024]{1,0:T(8,128)(2,1)} %param.12, f32[1024]{0:T(1024)} %param.13, f32[128]{0:T(128)S(1)} %add_rsqrt_fusion, f32[128]{0:T(128)S(1)} %broadcast_multiply_fusion), kind=kOutput, calls=%fused_computation.37 | convolution fusion | flops 537788416 | bytes 4985856 | tf_op jit(solution)/shard_map/dot_general | solution.py:38
  13.0 1.2 convolution_convert_fusion.3
  14.2 1.0 copy.100
  15.3 5.2 %all-to-all-start = ((bf16[1,1,4,4,128,128]{4,5,3,1,0,2:T(8,128)(2,1)}), bf16[1,1,4,4,128,128]{4,5,3,1,0,2:T(8,128)(2,1)}, u32[]{:S(2)}, u32[]{:S(2)}) async-start(bf16[1,1,4,4,128,128]{4,5,3,1,0,2:T(8,128)(2,1)} %copy.100), calls=%async_computation | async-start | bytes 1048576 | tf_op jit(solution)/shard_map/all_to_all | solution.py:42
  20.7 33.5 %all-gather.5.cloned.1.call-done = bf16[512,2048]{1,0:T(8,128)(2,1)} async-done(((bf16[128,2048]{1,0:T(8,128)(2,1)}), bf16[512,2048]{1,0:T(8,128)(2,1)}) %all-gather.5.cloned.1.call-update) | async-done | bytes 2097168 | tf_op jit(solution)/shard_map/all_gather | solution.py:41
  54.2 4.6 %reshape.131 = bf16[4,262144]{1,0:T(4,128)(2,1)} reshape(bf16[512,2048]{1,0:T(8,128)(2,1)} %all-gather.5.cloned.1.call-done) | data formatting | bytes 4194304 | tf_op jit(solution)/shard_map/reshape | solution.py:54
  58.8 26.2 %all-gather.3.cloned.1.call-done = bf16[1024,1024]{1,0:T(8,128)(2,1)} async-done(((bf16[128,1024]{1,0:T(8,128)(2,1)}), bf16[1024,1024]{1,0:T(8,128)(2,1)}) %all-gather.3.cloned.1.call-update) | async-done | bytes 2097168 | tf_op jit(solution)/shard_map/all_gather | solution.py:37
  85.0 3.8 %reshape.130 = bf16[8,131072]{1,0:T(8,128)(2,1)} reshape(bf16[1024,1024]{1,0:T(8,128)(2,1)} %all-gather.3.cloned.1.call-done) | data formatting | bytes 4194304 | tf_op jit(solution)/shard_map/reshape | solution.py:52
  88.8 80.2 %while.15 = (s32[]{:T(128)}, f32[4,4,8,128]{3,1,0,2:T(4,128)S(1)}, f32[4,4,8,128]{3,1,0,2:T(4,128)}, f32[4,4,128,8,128]{2,4,3,1,0:T(8,128)}, s32[4,4]{1,0:T(4,12...) while((s32[]{:T(128)}, f32[4,4,8,128]{3,1,0,2:T(4,128)S(1)}, ...), condition=%wide.region_5.6_spmd.clone, body=%wide.region_2.5_spmd.clone.sunk | while | flops 496033856 | bytes 54004036 | solution.py:99
  88.8 2.9 fusion.71
  92.0 1.4 fusion.72
  93.4 1.0 dynamic-slice_bitcast_fusion.2
  94.4 2.6 fusion.69
  97.0 1.9 copy.161
  98.8 2.5 fusion.74
  101.5 0.9 bitcast_convert_fusion.2
  102.5 0.9 fusion.75
  103.4 1.5 copy.164
  104.9 3.0 bitcast_dynamic-update-slice_fusion.2
  108.9 2.9 fusion.71
  112.1 1.4 fusion.72
  113.4 1.0 dynamic-slice_bitcast_fusion.2
  114.4 2.6 fusion.69
  117.0 1.9 copy.161
  118.9 2.5 fusion.74
  121.5 0.9 bitcast_convert_fusion.2
  122.5 0.9 fusion.75
  123.4 1.5 copy.164
  124.9 3.0 bitcast_dynamic-update-slice_fusion.2
  128.9 2.9 fusion.71
  132.1 1.4 fusion.72
  133.4 1.0 dynamic-slice_bitcast_fusion.2
  134.4 2.6 fusion.69
  137.0 1.9 copy.161
  138.9 2.5 fusion.74
  141.5 0.9 bitcast_convert_fusion.2
  142.5 0.9 fusion.75
  143.4 1.5 copy.164
  144.9 3.0 bitcast_dynamic-update-slice_fusion.2
  148.9 2.9 fusion.71
  152.1 1.4 fusion.72
  153.5 1.0 dynamic-slice_bitcast_fusion.2
  154.4 2.6 fusion.69
  157.0 1.9 copy.161
  158.9 2.5 fusion.74
  161.6 0.9 bitcast_convert_fusion.2
  162.5 0.9 fusion.75
  163.5 1.5 copy.164
  165.0 3.0 bitcast_dynamic-update-slice_fusion.2
  169.4 1.0 convolution_bitcast_fusion
  171.2 1.9 reduce.8
  173.1 0.9 reshape.155
  174.0 3.3 %all-to-all-start.3 = ((f32[8,1,1024]{2,1,0:T(1,128)}), f32[8,1,1024]{2,1,0:T(1,128)S(1)}, u32[]{:S(2)}, u32[]{:S(2)}) async-start(f32[8,1,1024]{2,1,0:T(1,128)} %reshape.155), calls=%async_computation.3 | async-start | bytes 65536 | tf_op jit(solution)/shard_map/all_to_all | solution.py:130
  177.7 1.9 reduce.10
  180.7 9.2 %copy.109 = f32[16,128,8,128]{3,0,2,1:T(8,128)} copy(f32[16,128,8,128]{1,3,2,0:T(8,128)} %bitcast.122) | data formatting | bytes 16777216 | tf_op jit(solution)/shard_map/reshape | solution.py:110
  189.9 5.0 %all-to-all-start.1 = ((f32[8,1,1024]{2,1,0:T(1,128)}), f32[8,1,1024]{2,1,0:T(1,128)S(1)}, u32[]{:S(2)}, u32[]{:S(2)}) async-start(f32[8,1,1024]{2,1,0:T(1,128)} %reshape.153), calls=%async_computation.1 | async-start | bytes 65536 | tf_op jit(solution)/shard_map/all_to_all | solution.py:129
  194.9 7.4 %fusion.19 = f32[8,128,8,128]{3,0,2,1:T(8,128)S(1)} fusion(f32[16,128,8,128]{3,0,2,1:T(8,128)} %copy.109, f32[16,128,8]{0,2,1:T(8,128)S(1)} %copy.108, s32[16]{0:T(128)S(1)} %get-tuple-element.149), kind=kOutput, calls=%fused_computation.33 | convolution fusion | flops 203423872 | bytes 12648512 | tf_op jit(solution)/shard_map/qs,sihd->qihd/dot_general | solution.py:118
  202.3 2.7 copy.110
  205.0 5.1 %all-to-all-start.2 = ((f32[1,1024,8,128]{3,2,0,1:T(8,128)}), f32[1,1024,8,128]{3,2,0,1:T(8,128)}, u32[]{:S(2)}, u32[]{:S(2)}) async-start(f32[1,1024,8,128]{3,2,0,1:T(8,128)} %bitcast.121), calls=%async_computation.2 | async-start | bytes 8388608 | tf_op jit(solution)/shard_map/all_to_all | solution.py:131
  214.0 90.2 %all-to-all-done.2 = f32[1,1024,8,128]{3,2,0,1:T(8,128)} async-done(((f32[1,1024,8,128]{3,2,0,1:T(8,128)}), f32[1,1024,8,128]{3,2,0,1:T(8,128)}, u32[]{:S(2)}, u32[]{:S(2)}) %all-to-all-start.2) | async-done | bytes 4194336 | tf_op jit(solution)/shard_map/all_to_all | solution.py:131
  304.2 3.0 multiply_reduce_fusion
  307.5 1.2 fusion.22
  (96 shorter events, 12.6 us)
Async XLA Ops:
  6.5 6.5 %copy-start = (bf16[1024,1024]{1,0:T(8,128)(2,1)S(1)}, bf16[1024,1024]{1,0:T(8,128)(2,1)}, u32[]{:S(2)}) copy-start(bf16[1024,1024]{1,0:T(8,128)(2,1)} %param.14) | copy-start | bytes 6291460
  6.5 47.6 %all-gather.5.cloned.1.call-start = ((), (), s32[]{:S(2)}) async-start(), calls=%async_computation.5 | async-start | bytes 2621440 | tf_op jit(solution)/shard_map/all_gather | solution.py:41
  8.9 4.1 %copy-start.4 = (bf16[128,1024]{1,0:T(8,128)(2,1)S(1)}, bf16[128,1024]{1,0:T(8,128)(2,1)}, u32[]{:S(2)}) copy-start(bf16[128,1024]{1,0:T(8,128)(2,1)} %param.12) | copy-start | bytes 786436
  9.0 4.1 %copy-start.8 = (f32[1024]{0:T(1024)S(1)}, f32[1024]{0:T(1024)}, u32[]{:S(2)}) copy-start(f32[1024]{0:T(1024)} %param.13) | copy-start | bytes 12292
  12.9 1.3 copy-start.6
  12.9 7.6 %copy-start.10 = (s32[1,1,2,16]{3,2,1,0:T(2,128)S(1)}, s32[1,1,2,16]{3,2,1,0:T(2,128)}, u32[]{:S(2)}) copy-start(s32[1,1,2,16]{3,2,1,0:T(2,128)} %param.19) | copy-start | bytes 388
  12.9 72.0 %all-gather.3.cloned.1.call-start = ((), (), s32[]{:S(2)}) async-start(), calls=%async_computation.4 | async-start | bytes 2359296 | tf_op jit(solution)/shard_map/all_gather | solution.py:37
  15.3 73.5 %all-to-all-start = ((bf16[1,1,4,4,128,128]{4,5,3,1,0,2:T(8,128)(2,1)}), bf16[1,1,4,4,128,128]{4,5,3,1,0,2:T(8,128)(2,1)}, u32[]{:S(2)}, u32[]{:S(2)}) async-start(bf16[1,1,4,4,128,128]{4,5,3,1,0,2:T(8,128)(2,1)} %copy.100), calls=%async_computation | async-start | bytes 1048576 | tf_op jit(solution)/shard_map/all_to_all | solution.py:42
  58.8 30.0 %copy-start.7 = (f32[32,8]{0,1:T(8,128)S(1)}, f32[32,8]{0,1:T(8,128)}, u32[]{:S(2)}) copy-start(f32[32,8]{0,1:T(8,128)} %param.17) | copy-start | bytes 3076
  58.8 30.0 %copy-start.9 = (f32[8]{0:T(128)S(1)}, f32[8]{0:T(128)}, u32[]{:S(2)}) copy-start(f32[8]{0:T(128)} %param.18) | copy-start | bytes 100
  98.8 3.6 %copy-start.2 = (f32[4,128,128,8]{1,2,3,0:T(8,128)S(1)}, f32[4,128,128,8]{1,2,3,0:T(8,128)}, u32[]{:S(2)}) copy-start(f32[4,128,128,8]{1,2,3,0:T(8,128)} %copy.161) | copy-start | bytes 6291460 | tf_op jit(solution)/shard_map/while
  98.8 3.6 %copy-start.3 = (bf16[4,128,1,8,128]{4,3,2,1,0:T(8,128)(2,1)S(1)}, bf16[4,128,1,8,128]{4,3,2,1,0:T(8,128)(2,1)}, u32[]{:S(2)}) copy-start(bf16[4,128,1,8,128]{4,3,2,1,0:T(8,128)(2,1)} %get-tuple-element.229) | copy-start | bytes 3145732 | tf_op jit(solution)/shard_map/while
  118.9 3.6 %copy-start.2 = (f32[4,128,128,8]{1,2,3,0:T(8,128)S(1)}, f32[4,128,128,8]{1,2,3,0:T(8,128)}, u32[]{:S(2)}) copy-start(f32[4,128,128,8]{1,2,3,0:T(8,128)} %copy.161) | copy-start | bytes 6291460 | tf_op jit(solution)/shard_map/while
  118.9 3.6 %copy-start.3 = (bf16[4,128,1,8,128]{4,3,2,1,0:T(8,128)(2,1)S(1)}, bf16[4,128,1,8,128]{4,3,2,1,0:T(8,128)(2,1)}, u32[]{:S(2)}) copy-start(bf16[4,128,1,8,128]{4,3,2,1,0:T(8,128)(2,1)} %get-tuple-element.229) | copy-start | bytes 3145732 | tf_op jit(solution)/shard_map/while
  138.9 3.6 %copy-start.2 = (f32[4,128,128,8]{1,2,3,0:T(8,128)S(1)}, f32[4,128,128,8]{1,2,3,0:T(8,128)}, u32[]{:S(2)}) copy-start(f32[4,128,128,8]{1,2,3,0:T(8,128)} %copy.161) | copy-start | bytes 6291460 | tf_op jit(solution)/shard_map/while
  138.9 3.6 %copy-start.3 = (bf16[4,128,1,8,128]{4,3,2,1,0:T(8,128)(2,1)S(1)}, bf16[4,128,1,8,128]{4,3,2,1,0:T(8,128)(2,1)}, u32[]{:S(2)}) copy-start(bf16[4,128,1,8,128]{4,3,2,1,0:T(8,128)(2,1)} %get-tuple-element.229) | copy-start | bytes 3145732 | tf_op jit(solution)/shard_map/while
  158.9 3.6 %copy-start.2 = (f32[4,128,128,8]{1,2,3,0:T(8,128)S(1)}, f32[4,128,128,8]{1,2,3,0:T(8,128)}, u32[]{:S(2)}) copy-start(f32[4,128,128,8]{1,2,3,0:T(8,128)} %copy.161) | copy-start | bytes 6291460 | tf_op jit(solution)/shard_map/while
  158.9 3.6 %copy-start.3 = (bf16[4,128,1,8,128]{4,3,2,1,0:T(8,128)(2,1)S(1)}, bf16[4,128,1,8,128]{4,3,2,1,0:T(8,128)(2,1)}, u32[]{:S(2)}) copy-start(bf16[4,128,1,8,128]{4,3,2,1,0:T(8,128)(2,1)} %get-tuple-element.229) | copy-start | bytes 3145732 | tf_op jit(solution)/shard_map/while
  174.0 15.9 %all-to-all-start.3 = ((f32[8,1,1024]{2,1,0:T(1,128)}), f32[8,1,1024]{2,1,0:T(1,128)S(1)}, u32[]{:S(2)}, u32[]{:S(2)}) async-start(f32[8,1,1024]{2,1,0:T(1,128)} %reshape.155), calls=%async_computation.3 | async-start | bytes 65536 | tf_op jit(solution)/shard_map/all_to_all | solution.py:130
  189.9 15.1 %all-to-all-start.1 = ((f32[8,1,1024]{2,1,0:T(1,128)}), f32[8,1,1024]{2,1,0:T(1,128)S(1)}, u32[]{:S(2)}, u32[]{:S(2)}) async-start(f32[8,1,1024]{2,1,0:T(1,128)} %reshape.153), calls=%async_computation.1 | async-start | bytes 65536 | tf_op jit(solution)/shard_map/all_to_all | solution.py:129
  205.0 99.2 %all-to-all-start.2 = ((f32[1,1024,8,128]{3,2,0,1:T(8,128)}), f32[1,1024,8,128]{3,2,0,1:T(8,128)}, u32[]{:S(2)}, u32[]{:S(2)}) async-start(f32[1,1024,8,128]{3,2,0,1:T(8,128)} %bitcast.121), calls=%async_computation.2 | async-start | bytes 8388608 | tf_op jit(solution)/shard_map/all_to_all | solution.py:131
  304.2 3.3 %copy-start.5 = (bf16[1024,1024]{1,0:T(8,128)(2,1)S(1)}, bf16[1024,1024]{1,0:T(8,128)(2,1)}, u32[]{:S(2)}) copy-start(bf16[1024,1024]{1,0:T(8,128)(2,1)} %param.16) | copy-start | bytes 6291460
  304.2 4.4 %copy-start.1 = (bf16[1024,1024]{1,0:T(8,128)(2,1)S(1)}, bf16[1024,1024]{1,0:T(8,128)(2,1)}, u32[]{:S(2)}) copy-start(bf16[1024,1024]{1,0:T(8,128)(2,1)} %param.14) | copy-start | bytes 6291460
Sparse Core Ops, SparseCore 0:
  13.0 41.0 all-gather.4
  55.8 29.1 all-gather.2
where the time goes:
time: 317 us; the launch traced here: 315 us
  waiting for transfers between devices  150 us (47%)
  matrix products  62.6 us (20%)
  local copies, waits for them, and re-layouts  54 us (17%)
  starting transfers between devices  18.7 us (6%)
  other arithmetic  16.3 us (5%)
  between operations  13.6 us (4%)
    all_to_all x1, waiting for transfers between devices, local(): lax.all_to_all(out_rows[None], 'col', split_axis=1, concat_axis=0, tiled=...  90.2 us
    all_gather x1, waiting for transfers between devices, local(): key_group = lax.all_gather(key_value, 'row', axis=0, tiled=True)  33.5 us
    all_gather x1, waiting for transfers between devices, local(): query_range = lax.all_gather(queries, 'col', axis=0, tiled=True)  26.2 us
    dot_general x4, matrix products, score_slots(): jnp.einsum('shij,sjhd->sihd', prob_vals, value_sel, preferred_element_typ...  12 us
    dot_general x4, matrix products, score_slots(): jnp.dot(key_pick, key_flat, preferred_element_type=jnp.float32)  11.5 us
    dot_general x4, matrix products, score_slots(): jnp.einsum('sijb,bh->shij', bucket_hot, bias_table, precision=lax.Precisi...  10.4 us
    dot_general x4, matrix products, score_slots(): jnp.dot(query_pick, query_flat, preferred_element_type=jnp.float32)  9.99 us
    reshape x1, local copies, waits for them, and re-layouts, local(): weighted = weighted.reshape(slot_count, tile_size, head_count, head_dim)  9.18 us
  transfers between devices with their start and end apart: 6, of which 3 were waited for; matrix products, arithmetic and copies ran while one was open for 12% of the time, Pallas kernels for 0%

commit v1 on v0

--- a/solution.py
+++ b/solution.py
@@ -38,7 +38,14 @@
     key_value = jnp.dot(normalized, w_keyvalue, preferred_element_type=jnp.float32).astype(
         jnp.bfloat16
     )
-    key_group = lax.all_gather(key_value, "row", axis=0, tiled=True)
+    devices = lax.axis_size("row")
+    right = [(i, (i + 1) % devices) for i in range(devices)]
+    parts = [key_value]
+    for far in range(1, devices):
+        parts = [lax.ppermute(parts[0], "row", right), *parts]
+    whole = jnp.concatenate(parts, axis=0)
+    offset = (lax.axis_index("row") + 1) * parts[-1].shape[0]
+    key_group = jnp.roll(whole, offset, axis=0)
     arrived = lax.all_to_all(edge_weight, "row", split_axis=2, concat_axis=0, tiled=True)
     slot_count = arrived.shape[0] * arrived.shape[3]
     edge_values = arrived.reshape(slot_count, tile_size, tile_size)

time: 317 us -> 301 us (0.950)
  waiting for transfers between devices: 150 us -> 127 us
  starting transfers between devices: 18.7 us -> 22.4 us
    ppermute x0 -> x3, waiting for transfers between devices: none -> 37.1 us  [local(): parts = [lax.ppermute(parts[0], 'row', right), *parts]]
    all_gather x1 -> x0, waiting for transfers between devices: 33.5 us -> none  [local(): key_group = lax.all_gather(key_value, 'row', axis=0, tiled=True)]
    all_gather x1, waiting for transfers between devices: 26.2 us -> 0.01 us  [local(): query_range = lax.all_gather(queries, 'col', axis=0, tiled=True)]
    ppermute x0 -> x3, starting transfers between devices: none -> 3.8 us  [local(): parts = [lax.ppermute(parts[0], 'row', right), *parts]]
    unnamed x24 -> x29, local copies, waits for them, and re-layouts: 5.14 us -> 7.47 us
    while x28 -> x44, local copies, waits for them, and re-layouts: 7.73 us -> 7.76 us
  transfers between devices with their start and end apart: 6 -> 8, of which waited for: 3 -> 4; matrix products, arithmetic and copies ran while one was open for 12% -> 13% of each run, Pallas kernels for 0% -> 0%
where the time goes in v1:
time: 301 us; the launch traced here: 300 us
  waiting for transfers between devices  127 us (42%)
  matrix products  64.4 us (21%)
  local copies, waits for them, and re-layouts  55 us (18%)
  starting transfers between devices  22.4 us (7%)
  other arithmetic  16.3 us (5%)
  between operations  13.7 us (5%)
    all_to_all x1, waiting for transfers between devices, local(): lax.all_to_all(out_rows[None], 'col', split_axis=1, concat_axis=0, tiled=...  90.2 us
    ppermute x3, waiting for transfers between devices, local(): parts = [lax.ppermute(parts[0], 'row', right), *parts]  37.1 us
    dot_general x4, matrix products, score_slots(): jnp.dot(key_pick, key_flat, preferred_element_type=jnp.float32)  12.3 us
    dot_general x4, matrix products, score_slots(): jnp.einsum('shij,sjhd->sihd', prob_vals, value_sel, preferred_element_typ...  12.3 us
    dot_general x4, matrix products, score_slots(): jnp.einsum('sijb,bh->shij', bucket_hot, bias_table, precision=lax.Precisi...  10.4 us
    dot_general x4, matrix products, score_slots(): jnp.dot(query_pick, query_flat, preferred_element_type=jnp.float32)  9.99 us
    reshape x1, local copies, waits for them, and re-layouts, local(): weighted = weighted.reshape(slot_count, tile_size, head_count, head_dim)  9.18 us
    while x44, local copies, waits for them, and re-layouts  7.76 us
  transfers between devices with their start and end apart: 8, of which 4 were waited for; matrix products, arithmetic and copies ran while one was open for 13% of the time, Pallas kernels for 0%

profile of v1, /device:TPU:0, one launch (start us, length us, event | category | flops | bytes accessed | tf_op | source)
XLA Modules:
  0.0 299.6 jit_solution(17774593680715657817)
XLA Ops:
  6.6 1.2 convert_reduce_fusion.1
  7.8 1.2 fusion.28
  9.0 3.1 %convolution_convert_fusion.2 = bf16[128,2048]{1,0:T(8,128)(2,1)S(1)} fusion(bf16[1024,2048]{1,0:T(8,128)(2,1)} %param.15, bf16[128,1024]{1,0:T(8,128)(2,1)} %param.12, f32[1024]{0:T(1024)} %param.13, f32[128]{0:T(128)S(1)} %add_rsqrt_fusion, f32[128]{0:T(128)S(1)} %broadcast_multiply_fusion), kind=kOutput, calls=%fused_computation.37 | convolution fusion | flops 537788416 | bytes 4985856 | tf_op jit(solution)/shard_map/dot_general | solution.py:38
  12.1 3.0 %collective-permute-start = (bf16[128,2048]{1,0:T(8,128)(2,1)S(1)}, bf16[128,2048]{1,0:T(8,128)(2,1)}, u32[]{:S(2)}, u32[]{:S(2)}) collective-permute-start(bf16[128,2048]{1,0:T(8,128)(2,1)S(1)} %convolution_convert_fusion.2), channel_id=1, source_target_pairs={{0,8},{8,16},{16,24},{24,0},{1,9},{9,17},{17,25},{25,1},{2,10},{10... | collective-permute-start | bytes 1572872 | tf_op jit(solution)/shard_map/ppermute | solution.py:45
  15.1 1.2 convolution_convert_fusion.3
  16.4 11.8 %collective-permute-done = bf16[128,2048]{1,0:T(8,128)(2,1)} collective-permute-done((bf16[128,2048]{1,0:T(8,128)(2,1)S(1)}, bf16[128,2048]{1,0:T(8,128)(2,1)}, u32[]{:S(2)}, u32[]{:S(2)}) %collective-permute-start) | collective-permute-done | bytes 524320 | tf_op jit(solution)/shard_map/ppermute | solution.py:45
  28.9 1.0 copy.100
  29.9 3.7 %all-to-all-start = ((bf16[1,1,4,4,128,128]{4,5,3,1,0,2:T(8,128)(2,1)}), bf16[1,1,4,4,128,128]{4,5,3,1,0,2:T(8,128)(2,1)S(1)}, u32[]{:S(2)}, u32[]{:S(2)}) async-start(bf16[1,1,4,4,128,128]{4,5,3,1,0,2:T(8,128)(2,1)} %copy.100), calls=%async_computation | async-start | bytes 1048576 | tf_op jit(solution)/shard_map/all_to_all | solution.py:49
  33.6 10.5 %collective-permute-done.1 = bf16[128,2048]{1,0:T(8,128)(2,1)S(1)} collective-permute-done((bf16[128,2048]{1,0:T(8,128)(2,1)}, bf16[128,2048]{1,0:T(8,128)(2,1)S(1)}, u32[]{:S(2)}, u32[]{:S(2)}) %collective-permute-start.1) | collective-permute-done | bytes 524320 | tf_op jit(solution)/shard_map/ppermute | solution.py:45
  44.3 14.9 %collective-permute-done.2 = bf16[128,2048]{1,0:T(8,128)(2,1)S(1)} collective-permute-done((bf16[128,2048]{1,0:T(8,128)(2,1)S(1)}, bf16[128,2048]{1,0:T(8,128)(2,1)S(1)}, u32[]{:S(2)}, u32[]{:S(2)}) %collective-permute-start.2) | collective-permute-done | bytes 524320 | tf_op jit(solution)/shard_map/ppermute | solution.py:45
  59.3 1.1 constant_dynamic-update-slice_fusion.5
  60.5 1.1 constant_dynamic-update-slice_fusion.1
  61.8 2.9 reshape.131
  64.7 3.9 %reshape.130 = bf16[8,131072]{1,0:T(8,128)(2,1)} reshape(bf16[1024,1024]{1,0:T(8,128)(2,1)} %all-gather.2.cloned.1.call-done) | data formatting | bytes 4194304 | tf_op jit(solution)/shard_map/reshape | solution.py:59
  68.7 81.4 %while.15 = (s32[]{:T(128)}, f32[4,4,8,128]{3,1,0,2:T(4,128)S(1)}, f32[4,4,8,128]{3,1,0,2:T(4,128)}, f32[4,4,128,8,128]{2,4,3,1,0:T(8,128)}, s32[4,4]{1,0:T(4,12...) while((s32[]{:T(128)}, f32[4,4,8,128]{3,1,0,2:T(4,128)S(1)}, ...), condition=%wide.region_5.6_spmd.clone, body=%wide.region_2.5_spmd.clone.sunk | while | flops 496033856 | bytes 58198396 | solution.py:106
  68.9 3.1 %fusion.71 = bf16[1,4,2048,128]{3,1,2,0:T(4,128)(2,1)S(1)} fusion(bf16[4,262144]{1,0:T(4,128)(2,1)} %get-tuple-element.268, s32[4]{0:T(128)S(1)} %fusion.70), kind=kOutput, calls=%fused_computation.13.clone.1 | convolution fusion | flops 9437200 | bytes 4194320 | tf_op jit(solution)/shard_map/while/body/eval_jaxpr/dot_general | solution.py:79
  72.2 1.4 fusion.72
  73.6 1.0 dynamic-slice_bitcast_fusion.2
  74.6 2.6 fusion.69
  77.2 1.9 copy.161
  79.1 2.5 fusion.74
  81.7 0.9 bitcast_convert_fusion.2
  83.6 1.5 copy.164
  85.1 3.1 %bitcast_dynamic-update-slice_fusion.2 = f32[4,4,128,8,128]{2,4,3,1,0:T(8,128)} fusion(f32[4,4,128,8,128]{2,4,3,1,0:T(8,128)} %get-tuple-element.251, s32[]{:T(128)} %get-tuple-element.248, bf16[4,128,1,8,128]{1,4,3,0,2:T(8,128)(2,1)} %copy.164, f32[4,8,128,128]{2,3,1,0:T(8,128)S(1)} %get-tuple-element.230, f32[4,8,128]{2,1,0:T(8,128)S(1)} %get-tuple-element.231), kind=kOutput, calls=%fused_computation.8.clone.1 | convolution fusion | flops 135266304 | bytes 5259776 | tf_op jit(solution)/shard_map/while/body/eval_jaxpr/shij,sjhd->sihd/dot_general | solution.py:101
  89.2 3.1 %fusion.71 = bf16[1,4,2048,128]{3,1,2,0:T(4,128)(2,1)S(1)} fusion(bf16[4,262144]{1,0:T(4,128)(2,1)} %get-tuple-element.268, s32[4]{0:T(128)S(1)} %fusion.70), kind=kOutput, calls=%fused_computation.13.clone.1 | convolution fusion | flops 9437200 | bytes 4194320 | tf_op jit(solution)/shard_map/while/body/eval_jaxpr/dot_general | solution.py:79
  92.6 1.4 fusion.72
  93.9 1.0 dynamic-slice_bitcast_fusion.2
  94.9 2.6 fusion.69
  97.5 1.9 copy.161
  99.4 2.5 fusion.74
  102.0 0.9 bitcast_convert_fusion.2
  103.9 1.5 copy.164
  105.4 3.0 %bitcast_dynamic-update-slice_fusion.2 = f32[4,4,128,8,128]{2,4,3,1,0:T(8,128)} fusion(f32[4,4,128,8,128]{2,4,3,1,0:T(8,128)} %get-tuple-element.251, s32[]{:T(128)} %get-tuple-element.248, bf16[4,128,1,8,128]{1,4,3,0,2:T(8,128)(2,1)} %copy.164, f32[4,8,128,128]{2,3,1,0:T(8,128)S(1)} %get-tuple-element.230, f32[4,8,128]{2,1,0:T(8,128)S(1)} %get-tuple-element.231), kind=kOutput, calls=%fused_computation.8.clone.1 | convolution fusion | flops 135266304 | bytes 5259776 | tf_op jit(solution)/shard_map/while/body/eval_jaxpr/shij,sjhd->sihd/dot_general | solution.py:101
  109.4 3.1 %fusion.71 = bf16[1,4,2048,128]{3,1,2,0:T(4,128)(2,1)S(1)} fusion(bf16[4,262144]{1,0:T(4,128)(2,1)} %get-tuple-element.268, s32[4]{0:T(128)S(1)} %fusion.70), kind=kOutput, calls=%fused_computation.13.clone.1 | convolution fusion | flops 9437200 | bytes 4194320 | tf_op jit(solution)/shard_map/while/body/eval_jaxpr/dot_general | solution.py:79
  112.8 1.4 fusion.72
  114.2 1.0 dynamic-slice_bitcast_fusion.2
  115.1 2.6 fusion.69
  117.8 1.9 copy.161
  119.6 2.5 fusion.74
  122.3 0.9 bitcast_convert_fusion.2
  124.2 1.5 copy.164
  125.7 3.1 %bitcast_dynamic-update-slice_fusion.2 = f32[4,4,128,8,128]{2,4,3,1,0:T(8,128)} fusion(f32[4,4,128,8,128]{2,4,3,1,0:T(8,128)} %get-tuple-element.251, s32[]{:T(128)} %get-tuple-element.248, bf16[4,128,1,8,128]{1,4,3,0,2:T(8,128)(2,1)} %copy.164, f32[4,8,128,128]{2,3,1,0:T(8,128)S(1)} %get-tuple-element.230, f32[4,8,128]{2,1,0:T(8,128)S(1)} %get-tuple-element.231), kind=kOutput, calls=%fused_computation.8.clone.1 | convolution fusion | flops 135266304 | bytes 5259776 | tf_op jit(solution)/shard_map/while/body/eval_jaxpr/shij,sjhd->sihd/dot_general | solution.py:101
  129.7 3.1 %fusion.71 = bf16[1,4,2048,128]{3,1,2,0:T(4,128)(2,1)S(1)} fusion(bf16[4,262144]{1,0:T(4,128)(2,1)} %get-tuple-element.268, s32[4]{0:T(128)S(1)} %fusion.70), kind=kOutput, calls=%fused_computation.13.clone.1 | convolution fusion | flops 9437200 | bytes 4194320 | tf_op jit(solution)/shard_map/while/body/eval_jaxpr/dot_general | solution.py:79
  133.1 1.4 fusion.72
  134.5 1.0 dynamic-slice_bitcast_fusion.2
  135.5 2.6 fusion.69
  138.1 1.9 copy.161
  139.9 2.5 fusion.74
  142.6 0.9 bitcast_convert_fusion.2
  143.5 0.9 fusion.75
  144.5 1.5 copy.164
  146.0 3.1 %bitcast_dynamic-update-slice_fusion.2 = f32[4,4,128,8,128]{2,4,3,1,0:T(8,128)} fusion(f32[4,4,128,8,128]{2,4,3,1,0:T(8,128)} %get-tuple-element.251, s32[]{:T(128)} %get-tuple-element.248, bf16[4,128,1,8,128]{1,4,3,0,2:T(8,128)(2,1)} %copy.164, f32[4,8,128,128]{2,3,1,0:T(8,128)S(1)} %get-tuple-element.230, f32[4,8,128]{2,1,0:T(8,128)S(1)} %get-tuple-element.231), kind=kOutput, calls=%fused_computation.8.clone.1 | convolution fusion | flops 135266304 | bytes 5259776 | tf_op jit(solution)/shard_map/while/body/eval_jaxpr/shij,sjhd->sihd/dot_general | solution.py:101
  150.5 1.0 convolution_bitcast_fusion
  152.3 1.9 reduce.8
  155.1 4.8 %all-to-all-start.3 = ((f32[8,1,1024]{2,1,0:T(1,128)}), f32[8,1,1024]{2,1,0:T(1,128)S(1)}, u32[]{:S(2)}, u32[]{:S(2)}) async-start(f32[8,1,1024]{2,1,0:T(1,128)} %reshape.155), calls=%async_computation.3 | async-start | bytes 65536 | tf_op jit(solution)/shard_map/all_to_all | solution.py:137
  160.2 1.9 reduce.10
  163.2 9.2 %copy.109 = f32[16,128,8,128]{3,0,2,1:T(8,128)} copy(f32[16,128,8,128]{1,3,2,0:T(8,128)} %bitcast.122) | data formatting | bytes 16777216 | tf_op jit(solution)/shard_map/reshape | solution.py:117
  172.4 5.1 %all-to-all-start.1 = ((f32[8,1,1024]{2,1,0:T(1,128)}), f32[8,1,1024]{2,1,0:T(1,128)S(1)}, u32[]{:S(2)}, u32[]{:S(2)}) async-start(f32[8,1,1024]{2,1,0:T(1,128)} %reshape.153), calls=%async_computation.1 | async-start | bytes 65536 | tf_op jit(solution)/shard_map/all_to_all | solution.py:136
  177.5 7.4 %fusion.19 = f32[8,128,8,128]{3,0,2,1:T(8,128)S(1)} fusion(f32[16,128,8,128]{3,0,2,1:T(8,128)} %copy.109, f32[16,128,8]{0,2,1:T(8,128)S(1)} %copy.108, s32[16]{0:T(128)S(1)} %get-tuple-element.149), kind=kOutput, calls=%fused_computation.33 | convolution fusion | flops 203423872 | bytes 12648512 | tf_op jit(solution)/shard_map/qs,sihd->qihd/dot_general | solution.py:125
  184.9 2.7 copy.110
  187.6 5.1 %all-to-all-start.2 = ((f32[1,1024,8,128]{3,2,0,1:T(8,128)}), f32[1,1024,8,128]{3,2,0,1:T(8,128)}, u32[]{:S(2)}, u32[]{:S(2)}) async-start(f32[1,1024,8,128]{3,2,0,1:T(8,128)} %bitcast.121), calls=%async_computation.2 | async-start | bytes 8388608 | tf_op jit(solution)/shard_map/all_to_all | solution.py:138
  196.6 90.2 %all-to-all-done.2 = f32[1,1024,8,128]{3,2,0,1:T(8,128)} async-done(((f32[1,1024,8,128]{3,2,0,1:T(8,128)}), f32[1,1024,8,128]{3,2,0,1:T(8,128)}, u32[]{:S(2)}, u32[]{:S(2)}) %all-to-all-start.2) | async-done | bytes 4194336 | tf_op jit(solution)/shard_map/all_to_all | solution.py:138
  286.8 3.0 %multiply_reduce_fusion = f32[128,8,128]{2,1,0:T(8,128)S(1)} fusion(f32[8,128,8,128]{3,2,1,0:T(8,128)} %bitcast.14, f32[8,128,8]{2,1,0:T(8,128)S(1)} %copy.106), kind=kLoop, calls=%fused_computation.35 | loop fusion | flops 1966080 | bytes 4751360 | tf_op jit(solution)/shard_map/reduce_sum | solution.py:143
  290.0 2.7 fusion.22
  (122 shorter events, 17.4 us)
Async XLA Ops:
  6.5 8.6 %copy-start = (bf16[1024,1024]{1,0:T(8,128)(2,1)S(1)}, bf16[1024,1024]{1,0:T(8,128)(2,1)}, u32[]{:S(2)}) copy-start(bf16[1024,1024]{1,0:T(8,128)(2,1)} %param.14) | copy-start | bytes 6291460
  6.5 8.6 %copy-start.4 = (bf16[128,1024]{1,0:T(8,128)(2,1)S(1)}, bf16[128,1024]{1,0:T(8,128)(2,1)}, u32[]{:S(2)}) copy-start(bf16[128,1024]{1,0:T(8,128)(2,1)} %param.12) | copy-start | bytes 786436
  6.5 8.6 %copy-start.9 = (f32[1024]{0:T(1024)S(1)}, f32[1024]{0:T(1024)}, u32[]{:S(2)}) copy-start(f32[1024]{0:T(1024)} %param.13) | copy-start | bytes 12292
  6.5 22.3 %copy-start.7 = (bf16[1,1,4,4,128,128]{5,4,3,2,1,0:T(8,128)(2,1)S(1)}, bf16[1,1,4,4,128,128]{5,4,3,2,1,0:T(8,128)(2,1)}, u32[]{:S(2)}) copy-start(bf16[1,1,4,4,128,128]{5,4,3,2,1,0:T(8,128)(2,1)} %param.21) | copy-start | bytes 1572868
  6.5 58.2 %all-gather.2.cloned.1.call-start = ((), (), s32[]{:S(2)}) async-start(), calls=%async_computation.4 | async-start | bytes 2359296 | tf_op jit(solution)/shard_map/all_gather | solution.py:37
  9.0 24.6 %copy-start.11 = (s32[1,1,2,16]{3,2,1,0:T(2,128)S(1)}, s32[1,1,2,16]{3,2,1,0:T(2,128)}, u32[]{:S(2)}) copy-start(s32[1,1,2,16]{3,2,1,0:T(2,128)} %param.19) | copy-start | bytes 388
  12.1 16.0 %collective-permute-start = (bf16[128,2048]{1,0:T(8,128)(2,1)S(1)}, bf16[128,2048]{1,0:T(8,128)(2,1)}, u32[]{:S(2)}, u32[]{:S(2)}) collective-permute-start(bf16[128,2048]{1,0:T(8,128)(2,1)S(1)} %convolution_convert_fusion.2), channel_id=1, source_target_pairs={{0,8},{8,16},{16,24},{24,0},{1,9},{9,17},{17,25},{25,1},{2,10},{10... | collective-permute-start | bytes 1572872 | tf_op jit(solution)/shard_map/ppermute | solution.py:45
  28.1 15.9 %collective-permute-start.1 = (bf16[128,2048]{1,0:T(8,128)(2,1)}, bf16[128,2048]{1,0:T(8,128)(2,1)S(1)}, u32[]{:S(2)}, u32[]{:S(2)}) collective-permute-start(bf16[128,2048]{1,0:T(8,128)(2,1)} %collective-permute-done), channel_id=1, source_target_pairs={{0,8},{8,16},{16,24},{24,0},{1,9},{9,17},{17,25},{25,1},{2,10},{10... | collective-permute-start | bytes 1572872 | tf_op jit(solution)/shard_map/ppermute | solution.py:45
  29.9 38.7 %all-to-all-start = ((bf16[1,1,4,4,128,128]{4,5,3,1,0,2:T(8,128)(2,1)}), bf16[1,1,4,4,128,128]{4,5,3,1,0,2:T(8,128)(2,1)S(1)}, u32[]{:S(2)}, u32[]{:S(2)}) async-start(bf16[1,1,4,4,128,128]{4,5,3,1,0,2:T(8,128)(2,1)} %copy.100), calls=%async_computation | async-start | bytes 1048576 | tf_op jit(solution)/shard_map/all_to_all | solution.py:49
  44.1 15.1 %collective-permute-start.2 = (bf16[128,2048]{1,0:T(8,128)(2,1)S(1)}, bf16[128,2048]{1,0:T(8,128)(2,1)S(1)}, u32[]{:S(2)}, u32[]{:S(2)}) collective-permute-start(bf16[128,2048]{1,0:T(8,128)(2,1)S(1)} %collective-permute-done.1), channel_id=1, source_target_pairs={{0,8},{8,16},{16,24},{24,0},{1,9},{9,17},{17,25},{25,1},{2,10},{10... | collective-permute-start | bytes 1572872 | tf_op jit(solution)/shard_map/ppermute | solution.py:45
  61.8 6.9 %copy-start.8 = (f32[32,8]{0,1:T(8,128)S(1)}, f32[32,8]{0,1:T(8,128)}, u32[]{:S(2)}) copy-start(f32[32,8]{0,1:T(8,128)} %param.17) | copy-start | bytes 3076
  61.8 6.9 %copy-start.10 = (f32[8]{0:T(128)S(1)}, f32[8]{0:T(128)}, u32[]{:S(2)}) copy-start(f32[8]{0:T(128)} %param.18) | copy-start | bytes 100
  68.9 3.4 %copy-start.5 = (bf16[4,4,128,128]{2,3,1,0:T(8,128)(2,1)}, bf16[4,4,128,128]{2,3,1,0:T(8,128)(2,1)S(1)}, u32[]{:S(2)}) copy-start(bf16[4,4,128,128]{2,3,1,0:T(8,128)(2,1)S(1)} %get-tuple-element.272) | copy-start | bytes 1572868 | tf_op jit(solution)/shard_map/while
  79.1 3.6 %copy-start.2 = (f32[4,128,128,8]{1,2,3,0:T(8,128)S(1)}, f32[4,128,128,8]{1,2,3,0:T(8,128)}, u32[]{:S(2)}) copy-start(f32[4,128,128,8]{1,2,3,0:T(8,128)} %copy.161) | copy-start | bytes 6291460 | tf_op jit(solution)/shard_map/while
  79.1 3.6 %copy-start.3 = (bf16[4,128,1,8,128]{4,3,2,1,0:T(8,128)(2,1)S(1)}, bf16[4,128,1,8,128]{4,3,2,1,0:T(8,128)(2,1)}, u32[]{:S(2)}) copy-start(bf16[4,128,1,8,128]{4,3,2,1,0:T(8,128)(2,1)} %get-tuple-element.229) | copy-start | bytes 3145732 | tf_op jit(solution)/shard_map/while
  85.1 4.1 %copy-start.6 = (bf16[4,4,128,128]{2,3,1,0:T(8,128)(2,1)S(1)}, bf16[4,4,128,128]{2,3,1,0:T(8,128)(2,1)}, u32[]{:S(2)}) copy-start(bf16[4,4,128,128]{2,3,1,0:T(8,128)(2,1)} %copy-done.5) | copy-start | bytes 1572868 | tf_op jit(solution)/shard_map/while
  89.2 3.4 %copy-start.5 = (bf16[4,4,128,128]{2,3,1,0:T(8,128)(2,1)}, bf16[4,4,128,128]{2,3,1,0:T(8,128)(2,1)S(1)}, u32[]{:S(2)}) copy-start(bf16[4,4,128,128]{2,3,1,0:T(8,128)(2,1)S(1)} %get-tuple-element.272) | copy-start | bytes 1572868 | tf_op jit(solution)/shard_map/while
  99.4 3.6 %copy-start.2 = (f32[4,128,128,8]{1,2,3,0:T(8,128)S(1)}, f32[4,128,128,8]{1,2,3,0:T(8,128)}, u32[]{:S(2)}) copy-start(f32[4,128,128,8]{1,2,3,0:T(8,128)} %copy.161) | copy-start | bytes 6291460 | tf_op jit(solution)/shard_map/while
  99.4 3.6 %copy-start.3 = (bf16[4,128,1,8,128]{4,3,2,1,0:T(8,128)(2,1)S(1)}, bf16[4,128,1,8,128]{4,3,2,1,0:T(8,128)(2,1)}, u32[]{:S(2)}) copy-start(bf16[4,128,1,8,128]{4,3,2,1,0:T(8,128)(2,1)} %get-tuple-element.229) | copy-start | bytes 3145732 | tf_op jit(solution)/shard_map/while
  105.4 4.0 %copy-start.6 = (bf16[4,4,128,128]{2,3,1,0:T(8,128)(2,1)S(1)}, bf16[4,4,128,128]{2,3,1,0:T(8,128)(2,1)}, u32[]{:S(2)}) copy-start(bf16[4,4,128,128]{2,3,1,0:T(8,128)(2,1)} %copy-done.5) | copy-start | bytes 1572868 | tf_op jit(solution)/shard_map/while
  109.4 3.4 %copy-start.5 = (bf16[4,4,128,128]{2,3,1,0:T(8,128)(2,1)}, bf16[4,4,128,128]{2,3,1,0:T(8,128)(2,1)S(1)}, u32[]{:S(2)}) copy-start(bf16[4,4,128,128]{2,3,1,0:T(8,128)(2,1)S(1)} %get-tuple-element.272) | copy-start | bytes 1572868 | tf_op jit(solution)/shard_map/while
  119.6 3.6 %copy-start.2 = (f32[4,128,128,8]{1,2,3,0:T(8,128)S(1)}, f32[4,128,128,8]{1,2,3,0:T(8,128)}, u32[]{:S(2)}) copy-start(f32[4,128,128,8]{1,2,3,0:T(8,128)} %copy.161) | copy-start | bytes 6291460 | tf_op jit(solution)/shard_map/while
  119.6 3.6 %copy-start.3 = (bf16[4,128,1,8,128]{4,3,2,1,0:T(8,128)(2,1)S(1)}, bf16[4,128,1,8,128]{4,3,2,1,0:T(8,128)(2,1)}, u32[]{:S(2)}) copy-start(bf16[4,128,1,8,128]{4,3,2,1,0:T(8,128)(2,1)} %get-tuple-element.229) | copy-start | bytes 3145732 | tf_op jit(solution)/shard_map/while
  125.7 4.1 %copy-start.6 = (bf16[4,4,128,128]{2,3,1,0:T(8,128)(2,1)S(1)}, bf16[4,4,128,128]{2,3,1,0:T(8,128)(2,1)}, u32[]{:S(2)}) copy-start(bf16[4,4,128,128]{2,3,1,0:T(8,128)(2,1)} %copy-done.5) | copy-start | bytes 1572868 | tf_op jit(solution)/shard_map/while
  129.7 3.4 %copy-start.5 = (bf16[4,4,128,128]{2,3,1,0:T(8,128)(2,1)}, bf16[4,4,128,128]{2,3,1,0:T(8,128)(2,1)S(1)}, u32[]{:S(2)}) copy-start(bf16[4,4,128,128]{2,3,1,0:T(8,128)(2,1)S(1)} %get-tuple-element.272) | copy-start | bytes 1572868 | tf_op jit(solution)/shard_map/while
  139.9 3.6 %copy-start.2 = (f32[4,128,128,8]{1,2,3,0:T(8,128)S(1)}, f32[4,128,128,8]{1,2,3,0:T(8,128)}, u32[]{:S(2)}) copy-start(f32[4,128,128,8]{1,2,3,0:T(8,128)} %copy.161) | copy-start | bytes 6291460 | tf_op jit(solution)/shard_map/while
  139.9 3.6 %copy-start.3 = (bf16[4,128,1,8,128]{4,3,2,1,0:T(8,128)(2,1)S(1)}, bf16[4,128,1,8,128]{4,3,2,1,0:T(8,128)(2,1)}, u32[]{:S(2)}) copy-start(bf16[4,128,1,8,128]{4,3,2,1,0:T(8,128)(2,1)} %get-tuple-element.229) | copy-start | bytes 3145732 | tf_op jit(solution)/shard_map/while
  146.0 4.1 %copy-start.6 = (bf16[4,4,128,128]{2,3,1,0:T(8,128)(2,1)S(1)}, bf16[4,4,128,128]{2,3,1,0:T(8,128)(2,1)}, u32[]{:S(2)}) copy-start(bf16[4,4,128,128]{2,3,1,0:T(8,128)(2,1)} %copy-done.5) | copy-start | bytes 1572868 | tf_op jit(solution)/shard_map/while
  155.1 17.3 %all-to-all-start.3 = ((f32[8,1,1024]{2,1,0:T(1,128)}), f32[8,1,1024]{2,1,0:T(1,128)S(1)}, u32[]{:S(2)}, u32[]{:S(2)}) async-start(f32[8,1,1024]{2,1,0:T(1,128)} %reshape.155), calls=%async_computation.3 | async-start | bytes 65536 | tf_op jit(solution)/shard_map/all_to_all | solution.py:137
  172.4 15.2 %all-to-all-start.1 = ((f32[8,1,1024]{2,1,0:T(1,128)}), f32[8,1,1024]{2,1,0:T(1,128)S(1)}, u32[]{:S(2)}, u32[]{:S(2)}) async-start(f32[8,1,1024]{2,1,0:T(1,128)} %reshape.153), calls=%async_computation.1 | async-start | bytes 65536 | tf_op jit(solution)/shard_map/all_to_all | solution.py:136
  187.6 99.2 %all-to-all-start.2 = ((f32[1,1024,8,128]{3,2,0,1:T(8,128)}), f32[1,1024,8,128]{3,2,0,1:T(8,128)}, u32[]{:S(2)}, u32[]{:S(2)}) async-start(f32[1,1024,8,128]{3,2,0,1:T(8,128)} %bitcast.121), calls=%async_computation.2 | async-start | bytes 8388608 | tf_op jit(solution)/shard_map/all_to_all | solution.py:138
  286.8 6.0 %copy-start.1 = (bf16[1024,1024]{1,0:T(8,128)(2,1)S(1)}, bf16[1024,1024]{1,0:T(8,128)(2,1)}, u32[]{:S(2)}) copy-start(bf16[1024,1024]{1,0:T(8,128)(2,1)} %param.14) | copy-start | bytes 6291460
Sparse Core Ops, SparseCore 0:
  16.5 29.4 all-gather.1
